TPU v7x, 256 devices: a whole 4x4x8 slice. The times are simulated.
256 devices in a mesh: slab: 64 (over z, y, core), dom: 4 (over x).
Axes of the slice: x: 4, y: 4, z: 8, core: 2. Of those that a mesh axis runs over, the one named last changes fastest.
Arguments:
- base_cells: int32 [3, 65536], P(None, ('slab', 'dom')), may hold values from 0 to 511, as said below
- offsets: float32 [3, 65536], P(None, ('slab', 'dom')), may hold values from 0 to 1
- charges: float32 [65536], P(('slab', 'dom')), may hold values from -4 to 4
- bias_coupling: float32 [65536], P(('slab', 'dom')), may hold values from -4 to 4
- counts: int32 [256], P(('slab', 'dom')), may hold values from 128 to 256, as said below
- green: float32 [256, 512, 256], P(None, 'slab', 'dom'), as said below
Outputs:
- potential: float32 [256, 512, 512], P('slab', 'dom')
- gradient: float32 [65536], P(('slab', 'dom'))
Inputs may be any that keep to these rules, and one draw needn't show every extreme that they name: `base_cells`: an atom in slot a belongs to device a // 256, which is slab index (a // 256) // 4 and dom index (a // 256) % 4 of the mesh; its base cell has first coordinate in that slab's 4 planes, second coordinate in that dom index's 128 rows, third coordinate anywhere in 0..511. `counts`: A multiple of 128 of at least half of 256; equal to 256 on at least one device; a device's atoms fill its first slots. `green`: zero at the zero wavenumber and positive elsewhere.
All inputs are finite; a program needn't handle non-finite values.
Results may differ from a plain program's by a relative error of at most 0.000086.
Values sent between devices are 32-bit elements; how exact they have to be, the bound alone decides.
A program may use at most 64 MiB of HBM per device.

v0:
```python
import functools

import numpy as np
import jax
import jax.numpy as jnp
from jax import lax
from jax.experimental import pallas as pl
from jax.experimental.pallas import tpu as pltpu
from jax.sharding import PartitionSpec as P

XD = 4
NY = 512
NZ = 512
NX = 256
N_SLAB = 64
N_DOM = 4
ROWS = NY // N_DOM
KY = NY // N_SLAB
ATOMS = 256
C = 128
MESH = pl.DeviceIdType.MESH
F32 = jnp.float32
BF16 = jnp.bfloat16
EXTRA = 16


def halves(table):
    table = np.asarray(table, np.float32)
    high = table.astype(jnp.bfloat16)
    low = (table - high.astype(np.float32)).astype(jnp.bfloat16)
    return np.stack([high, low])


def constants():
    kz_local = NZ // 2 // N_DOM
    kz = np.arange(NZ // 2)
    angle = 2 * np.pi * ((kz[:, None] * np.arange(NZ)[None, :]) % NZ) / NZ
    fz = np.stack([np.cos(angle).reshape(N_DOM, kz_local, NZ), -np.sin(angle).reshape(N_DOM, kz_local, NZ)], 1)
    fz = fz.reshape(2 * kz_local * N_DOM, NZ)
    k = np.arange(256)
    even = 2 * np.pi * ((k[:, None] * k[None, :]) % 256) / 256
    odd = 2 * np.pi * ((k[:, None] * (2 * k[None, :] + 1)) % 512) / 512
    cs_even = np.concatenate([np.cos(even), np.sin(even)], 1)
    cs_odd = np.concatenate([np.cos(odd), np.sin(odd)], 1)
    t, s = np.arange(4)[:, None], np.arange(32)[None, :]
    back_even, back_odd = [], []
    for part in range(2):
        cols = (8 * s + 4 * part + t).reshape(-1)
        back_even.append(np.concatenate([np.cos(even)[:, cols], np.sin(even)[:, cols]], 1))
        back_odd.append(np.concatenate([np.cos(odd).T[:, cols], np.sin(odd).T[:, cols]], 1))
    return (
        halves(fz),
        halves(cs_even),
        halves(cs_odd),
        halves(np.stack(back_even)),
        halves(np.stack(back_odd)),
    )


def split(value):
    high = value.astype(BF16)
    low = (value - high.astype(F32)).astype(BF16)
    return high, low


NN = (((1,), (0,)), ((), ()))
NT = (((1,), (1,)), ((), ()))


def dot3(a, b, dims=NN):
    def dot(x, y):
        return lax.dot_general(x, y, dims, preferred_element_type=F32)

    return dot(a[0], b[0]) + (dot(a[0], b[1]) + dot(a[1], b[0]))


def spline_rows(frac):
    inner = 1.0 - frac
    square = frac * frac
    cube = square * frac
    return [
        inner * inner * inner * (1.0 / 6.0),
        (3.0 * cube - 6.0 * square + 4.0) * (1.0 / 6.0),
        (-3.0 * cube + 3.0 * square + 3.0 * frac + 1.0) * (1.0 / 6.0),
        cube * (1.0 / 6.0),
    ]


def hot(t, weights):
    out = jnp.where(t == 0, weights[0], 0.0)
    for step in range(1, 4):
        out = jnp.where(t == step, weights[step], out)
    return out


def turned(value, sign):
    lane = lax.broadcasted_iota(jnp.int32, (1, C), 1)
    factor = jnp.where(lane < C // 2, sign, -sign).astype(F32)
    parts = [pltpu.roll(value[:, i : i + C], C // 2, 1) * factor for i in range(0, value.shape[1], C)]
    return jnp.concatenate(parts, 1)


def stacked(value, sign):
    return split(jnp.concatenate([value, turned(value, sign)], 0))


def shifted_slab(s, k):
    z, y, c = s // 8, (s // 2) % 4, s % 2
    dz, dy, dc = k // 8, (k // 2) % 4, k % 2
    return ((z + dz) % 8) * 8 + ((y + dy) % 4) * 2 + (c + dc) % 2


def signal(target):
    pl.semaphore_signal(pltpu.get_barrier_semaphore(), inc=1, device_id=target, device_id_type=MESH)


def atoms_kernel(own_ref, out_ref, send_sem, recv_sem):
    s, d = lax.axis_index("slab"), lax.axis_index("dom")
    nxt, prv = (s + 1) % N_SLAB, (s + N_SLAB - 1) % N_SLAB
    for i in range(N_DOM):
        e = (d + i) % N_DOM
        signal((nxt, e))
        signal((prv, e))
        if i:
            signal((s, e))
    pl.semaphore_wait(pltpu.get_barrier_semaphore(), 3 * N_DOM - 1)
    copies = []
    for i in range(N_DOM):
        for g in range(2):
            if i == 0 and g == 0:
                continue
            copies.append(
                pltpu.make_async_remote_copy(
                    own_ref,
                    out_ref.at[g, d],
                    send_sem.at[g, i],
                    recv_sem.at[g, i],
                    device_id=(nxt if g else s, (d + i) % N_DOM),
                    device_id_type=MESH,
                )
            )
    for copy in copies:
        copy.start()
    out_ref[0, d] = own_ref[...]
    for copy in copies:
        copy.wait()


def main_kernel(
    atoms_ref, finish_ref, green_hbm, fz_hbm, even_hbm, odd_hbm, back_even_hbm, back_odd_hbm,
    pot_ref, grad_ref,
    green, fz, even_m, odd_m, back_even, back_odd,
    hot_z, wy_tab, wx_tab, grid_even, grid_odd, send1, recv1, send2, recv2, acc_even, acc_odd, send3, recv3,
    parts, parts_in,
    load_sem, send_sem, r1, r2, r3, r4,
):
    s, d = lax.axis_index("slab"), lax.axis_index("dom")
    nxt, prv = (s + 1) % N_SLAB, (s + N_SLAB - 1) % N_SLAB
    right, left = (d + 1) % N_DOM, (d + N_DOM - 1) % N_DOM

    def greet(k, carry):
        signal((shifted_slab(s, k), d))
        return carry

    lax.fori_loop(1, N_SLAB, greet, 0)
    for i in range(1, N_DOM):
        signal((s, (d + i) % N_DOM))
    signal((nxt, right))
    signal((prv, left))

    loads = [
        pltpu.make_async_copy(src, dst, load_sem.at[i])
        for i, (src, dst) in enumerate(
            [
                (fz_hbm, fz),
                (even_hbm, even_m),
                (odd_hbm, odd_m),
                (green_hbm, green),
                (back_even_hbm, back_even),
                (back_odd_hbm, back_odd),
            ]
        )
    ]
    for load in loads:
        load.start()

    grid_even[...] = jnp.zeros_like(grid_even)
    grid_odd[...] = jnp.zeros_like(grid_odd)
    row_z = lax.broadcasted_iota(jnp.int32, (NZ, ATOMS), 0)
    row = lax.broadcasted_iota(jnp.int32, (ROWS + EXTRA, ATOMS), 0)
    half = ROWS // 2
    row_y = jnp.where(
        row < ROWS,
        2 * (row % half) + row // half,
        ROWS + 2 * ((row - ROWS) % (EXTRA // 2)) + (row - ROWS) // (EXTRA // 2),
    )
    row_x = lax.broadcasted_iota(jnp.int32, (8, ATOMS), 0)
    loads[0].wait()
    mine = pl.ds(pl.multiple_of(d * C, C), C)
    fz_mine = (fz[0, mine], fz[1, mine])

    def spread(n, carry):
        i, g = n // 2, n % 2
        e = (d + i) % N_DOM
        data = atoms_ref[g, e]
        whole = data[0:3].astype(jnp.int32)
        hz = split(hot((row_z - whole[2:3]) & (NZ - 1), spline_rows(data[5:6])))
        hot_z[n, 0] = hz[0]
        hot_z[n, 1] = hz[1]
        wx = hot(row_x - whole[0:1] + XD * g, spline_rows(data[3:4]))
        wx_tab[n] = wx
        wy = hot(row_y - whole[1:2], spline_rows(data[4:5]))
        lines = dot3(fz_mine, hz) * data[6:7]
        scaled = split(jnp.concatenate([lines * wx[p : p + 1] for p in range(XD)], 0))
        out = dot3(split(wy), scaled, NT)
        here = pl.ds(pl.multiple_of(e * half, half), half)
        after = pl.ds(pl.multiple_of(((e + 1) % N_DOM) * half, half), EXTRA // 2)
        grid_even[here, :] += out[:half]
        grid_odd[here, :] += out[half:ROWS]
        grid_even[after, :] += out[ROWS : ROWS + EXTRA // 2]
        grid_odd[after, :] += out[ROWS + EXTRA // 2 :]
        return carry

    lax.fori_loop(0, 2 * N_DOM, spread, 0)

    loads[1].wait()
    loads[2].wait()
    for pair in range(2):
        lanes = slice(2 * C * pair, 2 * C * (pair + 1))
        a = dot3((even_m[0], even_m[1]), stacked(grid_even[:, lanes], 1.0))
        b = dot3((odd_m[0], odd_m[1]), stacked(grid_odd[:, lanes], 1.0))
        for first, value in ((0, a + b), (N_SLAB // 2, a - b)):
            for q in range(2):
                send1[first : first + N_SLAB // 2, 2 * pair + q] = value[:, C * q : C * (q + 1)].reshape(
                    N_SLAB // 2, KY, C
                )

    pl.semaphore_wait(pltpu.get_barrier_semaphore(), N_SLAB - 1 + N_DOM - 1 + 2)

    def post1(k, carry):
        t = shifted_slab(s, k)
        pltpu.make_async_remote_copy(
            send1.at[t],
            recv1.at[s],
            send_sem.at[0],
            r1,
            device_id=(t, d),
            device_id_type=MESH,
        ).start()
        return carry

    lax.fori_loop(1, N_SLAB, post1, 0)
    natural = lax.broadcasted_iota(jnp.int32, (ROWS, ATOMS), 0)
    for g in range(2):
        for first, size, e in ((0, ROWS, d), (ROWS, 8, left)):
            data = atoms_ref[g, e]
            base = data[1:2].astype(jnp.int32)
            wy_tab[g, first : first + size] = hot(first + natural[:size] - base, spline_rows(data[4:5]))
    recv1[s] = send1[s]
    loads[3].wait()
    others = pl.ds(0, N_SLAB - 1)
    pltpu.make_async_copy(recv1.at[others], recv1.at[others], r1).wait()

    lane = lax.broadcasted_iota(jnp.int32, (1, C), 1)
    zero_bin = jnp.logical_and(lane % (C // 2) == 0, d == 0)
    scale = jnp.where(zero_bin, 1.0, 2.0).astype(F32) * (1.0 / (NX * NY * NZ))
    flat1 = recv1.reshape(NX * KY, C)
    for part in range(2):

        def along_x(pair, carry):
            t = 4 * part + 2 * pair
            value = jnp.concatenate([flat1[pl.ds(t + q, NX, stride=KY), :] for q in range(2)], 1)
            spec = dot3((even_m[0], even_m[1]), stacked(value, 1.0))
            factor = []
            for q in range(2):
                f = green[pl.ds(t + q, NX, stride=KY), :]
                factor.append(jnp.concatenate([f, f], 1) * scale)
            spec = spec * jnp.concatenate(factor, 1)
            out = dot3((even_m[0], even_m[1]), stacked(spec, -1.0))
            for q in range(2):
                send2[part, pl.ds(2 * pair + q, NX, stride=4), :] = out[:, C * q : C * (q + 1)]
            return carry

        lax.fori_loop(0, 2, along_x, 0)

        def post2(k, carry):
            t = shifted_slab(s, k)
            pltpu.make_async_remote_copy(
                send2.at[part, pl.ds(pl.multiple_of(t * 16, 16), 16)],
                recv2.at[part, pl.ds(pl.multiple_of(s * 16, 16), 16)],
                send_sem.at[1],
                r2.at[part],
                device_id=(t, d),
                device_id_type=MESH,
            ).start()
            return carry

        lax.fori_loop(1, N_SLAB, post2, 0)
        own = pl.ds(pl.multiple_of(s * 16, 16), 16)
        recv2[part, own, :] = send2[part, own, :]

    loads[4].wait()
    loads[5].wait()
    copies3 = []
    for part in range(2):
        rows = pl.ds(0, (N_SLAB - 1) * 16)
        pltpu.make_async_copy(recv2.at[part, rows], recv2.at[part, rows], r2.at[part]).wait()
        for pair in range(2):
            low, high = [], []
            for q in range(2):
                p = 2 * pair + q
                pick = [recv2[part, pl.ds(4 * p + t, N_SLAB, stride=16), :] for t in range(4)]
                low.append(jnp.concatenate([v[: N_SLAB // 2] for v in pick], 0))
                high.append(jnp.concatenate([v[N_SLAB // 2 :] for v in pick], 0))
            low, high = jnp.concatenate(low, 1), jnp.concatenate(high, 1)
            even = dot3((back_even[0, part], back_even[1, part]), stacked(low + high, -1.0))
            odd = dot3((back_odd[0, part], back_odd[1, part]), stacked(low - high, -1.0))
            if part == 0:
                acc_even[pair] = even
                acc_odd[pair] = odd
                continue
            even = even + acc_even[pair]
            odd = odd + acc_odd[pair]
            for q in range(2):
                lanes = slice(C * q, C * (q + 1))
                for e in range(N_DOM):
                    send3[pair, e, q, pl.ds(0, half, stride=2), :] = even[e * half : (e + 1) * half, lanes]
                    send3[pair, e, q, pl.ds(1, half, stride=2), :] = odd[e * half : (e + 1) * half, lanes]
            for i in range(1, N_DOM):
                e = (d + i) % N_DOM
                copy = pltpu.make_async_remote_copy(
                    send3.at[pair, e],
                    recv3.at[pair, d],
                    send_sem.at[2],
                    r3.at[pair],
                    device_id=(s, e),
                    device_id_type=MESH,
                )
                copy.start()
            recv3[pair, d] = send3[pair, d]

    totals = [jnp.zeros((1, ATOMS), F32) for _ in range(4)]
    for pair in range(2):
        three = pl.ds(0, N_DOM - 1)
        pltpu.make_async_copy(recv3.at[pair, three], recv3.at[pair, three], r3.at[pair]).wait()
        columns = jnp.concatenate([recv3[pair, e].reshape(2 * ROWS, C) for e in range(N_DOM)], 1)
        block = dot3(split(columns), (fz[0], fz[1]))
        for q in range(2):
            pot_ref[2 * pair + q] = block[q * ROWS : (q + 1) * ROWS]
        both = split(block)
        edge = split(jnp.concatenate([block[q * ROWS : q * ROWS + 8] for q in range(2)], 0))
        for g in range(2):
            u = dot3(both, (hot_z[g, 0], hot_z[g, 1]))
            v = dot3(edge, (hot_z[6 + g, 0], hot_z[6 + g, 1]))
            for q in range(2):
                p = 2 * pair + q
                here = jnp.sum(u[q * ROWS : (q + 1) * ROWS] * wy_tab[g, :ROWS], 0, keepdims=True)
                there = jnp.sum(v[q * 8 : (q + 1) * 8] * wy_tab[g, ROWS:], 0, keepdims=True)
                totals[2 * g] += here * wx_tab[g, p : p + 1]
                totals[2 * g + 1] += there * wx_tab[6 + g, p : p + 1]
    for n in range(1, 4):
        parts[n] = jnp.broadcast_to(totals[n], (8, ATOMS))
    for n, target in ((1, (s, left)), (2, (prv, d)), (3, (prv, left))):
        pltpu.make_async_remote_copy(
            parts.at[n], parts_in.at[n], send_sem.at[2 + n], r4.at[n], device_id=target, device_id_type=MESH
        ).start()
    for n in range(1, 4):
        pltpu.make_async_copy(parts_in.at[n], parts_in.at[n], r4.at[n]).wait()
    total = totals[0] + parts_in[1, 0:1] + parts_in[2, 0:1] + parts_in[3, 0:1]
    grad_ref[...] = finish_ref[...] * total

    pltpu.make_async_copy(send1.at[others], send1.at[others], send_sem.at[0]).wait()
    sent = pl.ds(0, (N_SLAB - 1) * 16)
    for part in range(2):
        pltpu.make_async_copy(send2.at[part, sent], send2.at[part, sent], send_sem.at[1]).wait()
    for pair in range(2):
        pltpu.make_async_copy(send3.at[pair, three], send3.at[pair, three], send_sem.at[2]).wait()
    for n in range(1, 4):
        pltpu.make_async_copy(parts.at[n], parts.at[n], send_sem.at[2 + n]).wait()


def per_device(base_cells, offsets, charges, bias_coupling, counts, green):
    alive = jnp.arange(ATOMS, dtype=jnp.int32) < counts[0]
    own = jnp.stack(
        [
            (base_cells[0] % XD).astype(F32),
            (base_cells[1] % ROWS).astype(F32),
            base_cells[2].astype(F32),
            offsets[0],
            offsets[1],
            offsets[2],
            jnp.where(alive, charges, 0.0),
            jnp.zeros_like(charges),
        ]
    )
    vmem = pl.BlockSpec(memory_space=pltpu.VMEM)
    anywhere = pl.BlockSpec(memory_space=pl.ANY)
    atoms = pl.pallas_call(
        atoms_kernel,
        out_shape=jax.ShapeDtypeStruct((2, N_DOM, 8, ATOMS), F32),
        in_specs=[vmem],
        out_specs=vmem,
        scratch_shapes=[pltpu.SemaphoreType.DMA((2, N_DOM)), pltpu.SemaphoreType.DMA((2, N_DOM))],
        compiler_params=pltpu.CompilerParams(collective_id=1, has_side_effects=True),
        name="atoms",
    )(own)
    finish = jnp.broadcast_to(jnp.where(alive, bias_coupling, 0.0)[None], (1, ATOMS))
    tables = [jnp.asarray(t) for t in constants()]
    potential, gradient = pl.pallas_call(
        main_kernel,
        out_shape=(
            jax.ShapeDtypeStruct((XD, ROWS, NZ), F32),
            jax.ShapeDtypeStruct((1, ATOMS), F32),
        ),
        in_specs=[vmem, vmem] + [anywhere] * 6,
        out_specs=(vmem, vmem),
        scratch_shapes=[
            pltpu.VMEM((NX * KY, C // 2), F32),
            *[pltpu.VMEM(t.shape, BF16) for t in tables],
            pltpu.VMEM((2 * N_DOM, 2, NZ, ATOMS), BF16),
            pltpu.VMEM((2, ROWS + 8, ATOMS), F32),
            pltpu.VMEM((2 * N_DOM, 8, ATOMS), F32),
            pltpu.VMEM((NY // 2, XD * C), F32),
            pltpu.VMEM((NY // 2, XD * C), F32),
            pltpu.VMEM((N_SLAB, XD, KY, C), F32),
            pltpu.VMEM((N_SLAB, XD, KY, C), F32),
            pltpu.VMEM((2, N_SLAB * 16, C), F32),
            pltpu.VMEM((2, N_SLAB * 16, C), F32),
            pltpu.VMEM((2, NY // 2, 2 * C), F32),
            pltpu.VMEM((2, NY // 2, 2 * C), F32),
            pltpu.VMEM((2, N_DOM, 2, ROWS, C), F32),
            pltpu.VMEM((2, N_DOM, 2, ROWS, C), F32),
            pltpu.VMEM((4, 8, ATOMS), F32),
            pltpu.VMEM((4, 8, ATOMS), F32),
            pltpu.SemaphoreType.DMA((6,)),
            pltpu.SemaphoreType.DMA((6,)),
            pltpu.SemaphoreType.DMA,
            pltpu.SemaphoreType.DMA((2,)),
            pltpu.SemaphoreType.DMA((2,)),
            pltpu.SemaphoreType.DMA((4,)),
        ],
        compiler_params=pltpu.CompilerParams(
            collective_id=2, has_side_effects=True, vmem_limit_bytes=48 * 1024 * 1024
        ),
        name="mesh",
    )(atoms, finish, green.reshape(NX * KY, C // 2), *tables)
    return (potential, gradient.reshape(ATOMS))


def solution(mesh):
    placed = (
        P(None, ("slab", "dom")),
        P(None, ("slab", "dom")),
        P(("slab", "dom")),
        P(("slab", "dom")),
        P(("slab", "dom")),
        P(None, "slab", "dom"),
    )
    return jax.shard_map(
        per_device,
        mesh=mesh,
        in_specs=placed,
        out_specs=(P("slab", "dom", None), P(("slab", "dom"))),
        check_vma=False,
    )
```

profile of v0, /device:TPU:1, one launch (start us, length us, event | category | flops | bytes accessed | tf_op | source)
XLA Modules:
  0.0 113.9 jit_solution(2231070315092534207)
XLA Ops:
  0.6 0.0 copy-start
  1.4 0.7 fusion.4
  2.1 0.8 slice_convert_fusion
  2.9 1.3 %stack.10.own_ref = f32[8,256]{1,0:T(8,128)} concatenate(f32[1,256]{1,0:T(1,128)S(1)} %get-tuple-element.7, f32[1,256]{1,0:T(1,128)S(1)} %get-tuple-element.8, f32[1,256]{1,0:T(1,128)S(1)} %get-tuple-element.6, f32[3,256]{1,0:T(4,128)} %param.12, f32[1,256]{1,0:T(1,128)S(1)} %bitcast.9, f32[1,256]{1,0:T(1,128)S(1)} %stack_broadcast_in_dim.3), dimensions={0} | concatenate | bytes 16384 | tf_op jit(solution)/shard_map/stack | solution.py:384
  4.2 15.8 %atoms.1.atoms_ref = f32[2,4,8,256]{3,2,1,0:T(8,128)} custom-call(f32[8,256]{1,0:T(8,128)} %stack.10.own_ref), custom_call_target="tpu_custom_call" | custom-call | tf_op jit(solution)/shard_map/atoms/pallas_call | solution.py:398
  20.0 0.0 copy-start.1
  20.0 0.0 copy-start.5
  20.0 1.5 %copy.13 = f32[256,8,64]{2,1,0:T(8,128)S(1)} copy(f32[256,8,64]{0,2,1:T(8,128)} %param.16) | data formatting | bytes 1048576 | tf_op args[5]
  21.6 0.0 copy-done
  21.6 0.0 copy-done.1
  21.6 0.0 copy-done.5
  21.6 0.0 copy-start.2
  21.6 1.0 copy-done.2
  22.6 0.0 copy-start.3
  22.6 1.0 copy-done.3
  23.7 0.0 copy-start.4
  23.7 1.0 copy-done.4
  24.7 87.6 %mesh.1 = (f32[4,128,512]{2,1,0:T(8,128)S(1)}, f32[1,256]{1,0:T(1,128)S(1)}) custom-call(f32[2,4,8,256]{3,2,1,0:T(8,128)S(1)} %copy-done.5, f32[1,256]{1,0:T(1,128)S(1)} %bitcast.7, f32[2048,64]{1,0:T(8,128)S(1)} %bitcast.6, bf16[2,512,512]{2,1,0:T(8,128)(2,1)S(1)} %copy-done, bf16[2,256,512]{2,1,0:T(8,128)(2,1)S(1)} %copy-done.4, ...), custom_call_target="tpu_custom_call" | custom-call | tf_op jit(solution)/shard_map/mesh/pallas_call | solution.py:409
  112.4 1.0 copy.17
  113.3 0.6 copy.18
  (1 shorter events, 0.0 us)
Async XLA Ops:
  0.6 20.9 %copy-start = (bf16[2,512,512]{2,1,0:T(8,128)(2,1)S(1)}, bf16[2,512,512]{2,1,0:T(8,128)(2,1)}, u32[]{:S(2)}) copy-start(bf16[2,512,512]{2,1,0:T(8,128)(2,1)} %constant.39.clone.fz_hbm) | copy-start | bytes 3145732
  20.0 1.6 %copy-start.1 = (bf16[2,2,256,256]{3,2,1,0:T(8,128)(2,1)S(1)}, bf16[2,2,256,256]{3,2,1,0:T(8,128)(2,1)}, u32[]{:S(2)}) copy-start(bf16[2,2,256,256]{3,2,1,0:T(8,128)(2,1)} %constant.43.clone.back_odd_hbm) | copy-start | bytes 1572868
  20.0 1.6 %copy-start.5 = (f32[2,4,8,256]{3,2,1,0:T(8,128)S(1)}, f32[2,4,8,256]{3,2,1,0:T(8,128)}, u32[]{:S(2)}) copy-start(f32[2,4,8,256]{3,2,1,0:T(8,128)} %atoms.1.atoms_ref) | copy-start | bytes 196612
  21.6 1.0 copy-start.2
  22.6 1.0 copy-start.3
  23.7 1.0 copy-start.4
where the time goes:
time: 114 us
  Pallas kernels  103 us (90%)
  local copies, waits for them, and re-layouts  7.51 us (7%)
  other arithmetic  1.51 us (1%)
  between operations  1.46 us (1%)
    pallas_call x1, Pallas kernels, per_device(): pl.pallas_call(main_kernel, out_shape=(jax.ShapeDtypeStruct((XD, ROWS, NZ...  87.6 us
    pallas_call x1, Pallas kernels, per_device(): pl.pallas_call(atoms_kernel, out_shape=jax.ShapeDtypeStruct((2, N_DOM, 8,...  15.8 us
    unnamed x15, local copies, waits for them, and re-layouts  6.2 us

commit v1 on v0

v1 whole, which is shorter than its diff:
```python
import functools

import numpy as np
import jax
import jax.numpy as jnp
from jax import lax
from jax.experimental import pallas as pl
from jax.experimental.pallas import tpu as pltpu
from jax.sharding import PartitionSpec as P

XD = 4
NY = 512
NZ = 512
NX = 256
N_SLAB = 64
N_DOM = 4
ROWS = NY // N_DOM
KY = NY // N_SLAB
ATOMS = 256
C = 128
MESH = pl.DeviceIdType.MESH
F32 = jnp.float32
BF16 = jnp.bfloat16
CHUNK = 1
CHUNKS = XD // CHUNK
EXTRA = 16


def halves(table):
    table = np.asarray(table, np.float32)
    high = table.astype(jnp.bfloat16)
    low = (table - high.astype(np.float32)).astype(jnp.bfloat16)
    return np.stack([high, low])


def constants():
    kz_local = NZ // 2 // N_DOM
    kz = np.arange(NZ // 2)
    angle = 2 * np.pi * ((kz[:, None] * np.arange(NZ)[None, :]) % NZ) / NZ
    fz = np.stack([np.cos(angle).reshape(N_DOM, kz_local, NZ), -np.sin(angle).reshape(N_DOM, kz_local, NZ)], 1)
    fz = fz.reshape(2 * kz_local * N_DOM, NZ)
    k = np.arange(256)
    even = 2 * np.pi * ((k[:, None] * k[None, :]) % 256) / 256
    odd = 2 * np.pi * ((k[:, None] * (2 * k[None, :] + 1)) % 512) / 512
    cs_even = np.concatenate([np.cos(even), np.sin(even)], 1)
    cs_odd = np.concatenate([np.cos(odd), np.sin(odd)], 1)
    cs_odd_t = np.concatenate([np.cos(odd).T, np.sin(odd).T], 1)
    return halves(np.concatenate([fz, cs_even, cs_odd, cs_odd_t], 0))


def split(value):
    high = value.astype(BF16)
    low = (value - high.astype(F32)).astype(BF16)
    return high, low


NN = (((1,), (0,)), ((), ()))
NT = (((1,), (1,)), ((), ()))


def dot3(a, b, dims=NN):
    def dot(x, y):
        return lax.dot_general(x, y, dims, preferred_element_type=F32)

    return dot(a[0], b[0]) + (dot(a[0], b[1]) + dot(a[1], b[0]))


def spline_rows(frac):
    inner = 1.0 - frac
    square = frac * frac
    cube = square * frac
    return [
        inner * inner * inner * (1.0 / 6.0),
        (3.0 * cube - 6.0 * square + 4.0) * (1.0 / 6.0),
        (-3.0 * cube + 3.0 * square + 3.0 * frac + 1.0) * (1.0 / 6.0),
        cube * (1.0 / 6.0),
    ]


def hot(t, weights):
    out = jnp.where(t == 0, weights[0], 0.0)
    for step in range(1, 4):
        out = jnp.where(t == step, weights[step], out)
    return out


def turned(value, sign):
    lane = lax.broadcasted_iota(jnp.int32, (1, C), 1)
    factor = jnp.where(lane < C // 2, sign, -sign).astype(F32)
    parts = [pltpu.roll(value[:, i : i + C], C // 2, 1) * factor for i in range(0, value.shape[1], C)]
    return jnp.concatenate(parts, 1)


def stacked(value, sign):
    return split(jnp.concatenate([value, turned(value, sign)], 0))


def shifted_slab(s, k):
    z, y, c = s // 8, (s // 2) % 4, s % 2
    dz, dy, dc = k // 8, (k // 2) % 4, k % 2
    return ((z + dz) % 8) * 8 + ((y + dy) % 4) * 2 + (c + dc) % 2


def signal(target):
    pl.semaphore_signal(pltpu.get_barrier_semaphore(), inc=1, device_id=target, device_id_type=MESH)


def main_kernel(
    counts_ref, cells_ref, offsets_ref, charges_ref, bias_ref, green_hbm, table_hbm,
    pot_ref, grad_ref,
    green, fz, even_m, odd_m, back_odd,
    own_ref, atoms_ref, factors, by_plane,
    hot_z, wy_tab, wx_tab, grid_even, grid_odd, send1, recv1, spectrum, send2, recv2, send3, recv3,
    totals, parts, parts_in,
    load_sem, send_sem, atom_send, atom_recv, r1, r2, r3, r4,
):
    s, d = lax.axis_index("slab"), lax.axis_index("dom")
    nxt, prv = (s + 1) % N_SLAB, (s + N_SLAB - 1) % N_SLAB
    right, left = (d + 1) % N_DOM, (d + N_DOM - 1) % N_DOM

    def greet(k, carry):
        signal((shifted_slab(s, k), d))
        return carry

    for i in range(1, N_DOM):
        signal((s, (d + i) % N_DOM))
        signal((nxt, (d + i) % N_DOM))
        signal((prv, (d + i) % N_DOM))
    lax.fori_loop(1, N_SLAB, greet, 0)

    loads = [
        pltpu.make_async_copy(src, dst, load_sem.at[i])
        for i, (src, dst) in enumerate(
            [
                (table_hbm.at[:, 0:NZ], fz),
                (table_hbm.at[:, NZ : NZ + NX], even_m),
                (table_hbm.at[:, NZ + NX : NZ + 2 * NX], odd_m),
                (green_hbm, green),
                (table_hbm.at[:, NZ + 2 * NX : NZ + 3 * NX], back_odd),
            ]
        )
    ]
    for load in loads:
        load.start()

    slot = lax.broadcasted_iota(jnp.int32, (1, ATOMS), 1)
    alive = slot < counts_ref[0]
    own_ref[0:1] = (cells_ref[0:1] % XD).astype(F32)
    own_ref[1:2] = (cells_ref[1:2] % ROWS).astype(F32)
    own_ref[2:3] = cells_ref[2:3].astype(F32)
    own_ref[3:6] = offsets_ref[...]
    own_ref[6:7] = jnp.where(alive, charges_ref[...], 0.0)
    own_ref[7:8] = jnp.zeros((1, ATOMS), F32)
    atoms_ref[0, d] = own_ref[...]
    grid_even[...] = jnp.zeros_like(grid_even)
    grid_odd[...] = jnp.zeros_like(grid_odd)
    totals[...] = jnp.zeros_like(totals)

    loads[1].wait()
    r = lax.broadcasted_iota(jnp.int32, (NX, NX), 0)
    x = lax.broadcasted_iota(jnp.int32, (NX, NX), 1)
    per = N_SLAB * CHUNK
    chosen = XD * ((r % per) // CHUNK) + CHUNK * (r // per) + r % CHUNK
    pick = jnp.where(x == chosen, 1.0, 0.0).astype(BF16)
    for n in range(2):
        by_plane[n] = lax.dot_general(pick, even_m[n], NN, preferred_element_type=F32).astype(BF16)

    loads[3].wait()
    lane = lax.broadcasted_iota(jnp.int32, (1, C), 1)
    zero_bin = jnp.logical_and(lane % (C // 2) == 0, d == 0)
    scale = jnp.where(zero_bin, 1.0, 2.0).astype(F32) * (1.0 / (NX * NY * NZ))

    def prepare(t, carry):
        f = green[t]
        factors[t] = jnp.concatenate([f, f], 0).T * scale
        return carry

    lax.fori_loop(0, KY, prepare, 0)

    pl.semaphore_wait(pltpu.get_barrier_semaphore(), N_SLAB - 1 + 3 * (N_DOM - 1))

    for g in range(2):
        for i in range(N_DOM):
            if i == 0 and g == 0:
                continue
            pltpu.make_async_remote_copy(
                own_ref,
                atoms_ref.at[g, d],
                atom_send,
                atom_recv.at[g, i],
                device_id=(nxt if g else s, (d + i) % N_DOM),
                device_id_type=MESH,
            ).start()

    row_z = lax.broadcasted_iota(jnp.int32, (NZ, ATOMS), 0)
    row = lax.broadcasted_iota(jnp.int32, (ROWS + EXTRA, ATOMS), 0)
    half = ROWS // 2
    row_y = jnp.where(
        row < ROWS,
        2 * (row % half) + row // half,
        ROWS + 2 * ((row - ROWS) % (EXTRA // 2)) + (row - ROWS) // (EXTRA // 2),
    )
    row_x = lax.broadcasted_iota(jnp.int32, (8, ATOMS), 0)
    loads[0].wait()
    mine = pl.ds(pl.multiple_of(d * C, C), C)
    fz_mine = (fz[0, mine], fz[1, mine])

    def spread(n, carry):
        i, g = n // 2, n % 2
        e = (d + i) % N_DOM

        @pl.when(n > 0)
        def _():
            block = atoms_ref.at[g, e]
            pltpu.make_async_copy(block, block, atom_recv.at[g, (N_DOM - i) % N_DOM]).wait()

        data = atoms_ref[g, e]
        whole = data[0:3].astype(jnp.int32)
        hz = split(hot((row_z - whole[2:3]) & (NZ - 1), spline_rows(data[5:6])))
        hot_z[n, 0] = hz[0]
        hot_z[n, 1] = hz[1]
        wx = hot(row_x - whole[0:1] + XD * g, spline_rows(data[3:4]))
        wx_tab[n] = wx
        wy = hot(row_y - whole[1:2], spline_rows(data[4:5]))
        lines = dot3(fz_mine, hz) * data[6:7]
        scaled = split(jnp.concatenate([lines * wx[p : p + 1] for p in range(XD)], 0))
        out = dot3(split(wy), scaled, NT)
        here = pl.ds(pl.multiple_of(e * half, half), half)
        after = pl.ds(pl.multiple_of(((e + 1) % N_DOM) * half, half), EXTRA // 2)
        grid_even[here, :] += out[:half]
        grid_odd[here, :] += out[half:ROWS]
        grid_even[after, :] += out[ROWS : ROWS + EXTRA // 2]
        grid_odd[after, :] += out[ROWS + EXTRA // 2 :]
        return carry

    lax.fori_loop(0, 2 * N_DOM, spread, 0)

    loads[2].wait()
    for pair in range(2):
        lanes = slice(2 * C * pair, 2 * C * (pair + 1))
        a = dot3((even_m[0], even_m[1]), stacked(grid_even[:, lanes], 1.0))
        b = dot3((odd_m[0], odd_m[1]), stacked(grid_odd[:, lanes], 1.0))
        for first, value in ((0, a + b), (N_SLAB // 2, a - b)):
            for q in range(2):
                send1[first : first + N_SLAB // 2, 2 * pair + q] = value[:, C * q : C * (q + 1)].reshape(
                    N_SLAB // 2, KY, C
                )

    def post1(k, carry):
        t = shifted_slab(s, k)
        pltpu.make_async_remote_copy(
            send1.at[t], recv1.at[s], send_sem.at[0], r1, device_id=(t, d), device_id_type=MESH
        ).start()
        return carry

    lax.fori_loop(1, N_SLAB, post1, 0)
    natural = lax.broadcasted_iota(jnp.int32, (ROWS, ATOMS), 0)
    for g in range(2):
        for first, size, e in ((0, ROWS, d), (ROWS, 8, left)):
            data = atoms_ref[g, e]
            base = data[1:2].astype(jnp.int32)
            wy_tab[g, first : first + size] = hot(first + natural[:size] - base, spline_rows(data[4:5]))
    recv1[s] = send1[s]
    others = pl.ds(0, N_SLAB - 1)
    pltpu.make_async_copy(recv1.at[others], recv1.at[others], r1).wait()

    flat1 = recv1.reshape(NX * KY, C)
    for pair in range(KY // 2):
        value = jnp.concatenate([flat1[pl.ds(2 * pair + q, NX, stride=KY), :] for q in range(2)], 1)
        spec = dot3((even_m[0], even_m[1]), stacked(value, 1.0))
        spec = spec * jnp.concatenate([factors[2 * pair], factors[2 * pair + 1]], 1)
        high, low = stacked(spec, -1.0)
        spectrum[0, :, 2 * C * pair : 2 * C * (pair + 1)] = high
        spectrum[1, :, 2 * C * pair : 2 * C * (pair + 1)] = low

    flat2 = send2.reshape(CHUNKS, per * KY, C)

    def along_x(ch, carry):
        rows = pl.ds(pl.multiple_of(ch * per, per), per)
        out = dot3((by_plane[0, rows], by_plane[1, rows]), (spectrum[0], spectrum[1]))
        for t in range(KY):
            flat2[ch, pl.ds(t, per, stride=KY), :] = out[:, C * t : C * (t + 1)]

        def post2(k, inner):
            t = shifted_slab(s, k)
            pltpu.make_async_remote_copy(
                send2.at[ch, t],
                recv2.at[ch, s],
                send_sem.at[1],
                r2.at[ch],
                device_id=(t, d),
                device_id_type=MESH,
            ).start()
            return inner

        lax.fori_loop(1, N_SLAB, post2, 0)
        recv2[ch, s] = send2[ch, s]
        return carry

    lax.fori_loop(0, CHUNKS, along_x, 0)
    loads[4].wait()
    three = pl.ds(0, N_DOM - 1)

    def finish(ch, carry):
        @pl.when(ch < CHUNKS)
        def _():
            pltpu.make_async_copy(recv2.at[ch, others], recv2.at[ch, others], r2.at[ch]).wait()
            value = jnp.concatenate([recv2[ch, :, q].reshape(NY, C) for q in range(CHUNK)], 1)
            low, high = value[: NY // 2], value[NY // 2 :]
            even = dot3((even_m[0], even_m[1]), stacked(low + high, -1.0))
            odd = dot3((back_odd[0], back_odd[1]), stacked(low - high, -1.0))
            for q in range(CHUNK):
                lanes = slice(C * q, C * (q + 1))
                for e in range(N_DOM):
                    send3[ch, e, q, pl.ds(0, half, stride=2), :] = even[e * half : (e + 1) * half, lanes]
                    send3[ch, e, q, pl.ds(1, half, stride=2), :] = odd[e * half : (e + 1) * half, lanes]
            for i in range(1, N_DOM):
                e = (d + i) % N_DOM
                pltpu.make_async_remote_copy(
                    send3.at[ch, e],
                    recv3.at[ch, d],
                    send_sem.at[2],
                    r3.at[ch],
                    device_id=(s, e),
                    device_id_type=MESH,
                ).start()
            recv3[ch, d] = send3[ch, d]

        @pl.when(ch > 0)
        def _():
            c = ch - 1
            pltpu.make_async_copy(recv3.at[c, three], recv3.at[c, three], r3.at[c]).wait()
            columns = jnp.concatenate([recv3[c, e].reshape(CHUNK * ROWS, C) for e in range(N_DOM)], 1)
            block = dot3(split(columns), (fz[0], fz[1]))
            for q in range(CHUNK):
                pot_ref[CHUNK * c + q] = block[q * ROWS : (q + 1) * ROWS]
            both = split(block)
            edge = split(jnp.concatenate([block[q * ROWS : q * ROWS + 8] for q in range(CHUNK)], 0))
            for g in range(2):
                u = dot3(both, (hot_z[g, 0], hot_z[g, 1]))
                v = dot3(edge, (hot_z[6 + g, 0], hot_z[6 + g, 1]))
                for q in range(CHUNK):
                    p = CHUNK * c + q
                    here = jnp.sum(u[q * ROWS : (q + 1) * ROWS] * wy_tab[g, :ROWS], 0, keepdims=True)
                    there = jnp.sum(v[q * 8 : (q + 1) * 8] * wy_tab[g, ROWS:], 0, keepdims=True)
                    totals[2 * g] += here * wx_tab[g, pl.ds(p, 1)]
                    totals[2 * g + 1] += there * wx_tab[6 + g, pl.ds(p, 1)]

        return carry

    lax.fori_loop(0, CHUNKS + 1, finish, 0)

    for n in range(1, 4):
        parts[n] = jnp.broadcast_to(totals[n], (8, ATOMS))
    for n, target in ((1, (s, left)), (2, (prv, d)), (3, (prv, left))):
        pltpu.make_async_remote_copy(
            parts.at[n], parts_in.at[n], send_sem.at[2 + n], r4.at[n], device_id=target, device_id_type=MESH
        ).start()
    for n in range(1, 4):
        pltpu.make_async_copy(parts_in.at[n], parts_in.at[n], r4.at[n]).wait()
    total = totals[0] + parts_in[1, 0:1] + parts_in[2, 0:1] + parts_in[3, 0:1]
    grad_ref[...] = jnp.where(alive, bias_ref[...] * total, 0.0)

    seven = atoms_ref.reshape(2 * N_DOM, 8, ATOMS).at[pl.ds(0, 2 * N_DOM - 1)]
    pltpu.make_async_copy(seven, seven, atom_send).wait()
    pltpu.make_async_copy(send1.at[others], send1.at[others], send_sem.at[0]).wait()

    def drain(ch, carry):
        pltpu.make_async_copy(send2.at[ch, others], send2.at[ch, others], send_sem.at[1]).wait()
        pltpu.make_async_copy(send3.at[ch, three], send3.at[ch, three], send_sem.at[2]).wait()
        return carry

    lax.fori_loop(0, CHUNKS, drain, 0)
    for n in range(1, 4):
        pltpu.make_async_copy(parts.at[n], parts.at[n], send_sem.at[2 + n]).wait()


def per_device(base_cells, offsets, charges, bias_coupling, counts, green):
    vmem = pl.BlockSpec(memory_space=pltpu.VMEM)
    hbm = pl.BlockSpec(memory_space=pltpu.HBM)
    potential, gradient = pl.pallas_call(
        main_kernel,
        out_shape=(
            jax.ShapeDtypeStruct((XD, ROWS, NZ), F32),
            jax.ShapeDtypeStruct((1, ATOMS), F32),
        ),
        in_specs=[pl.BlockSpec(memory_space=pltpu.SMEM)] + [vmem] * 4 + [hbm] * 2,
        out_specs=(vmem, vmem),
        scratch_shapes=[
            pltpu.VMEM((KY, C // 2, NX), F32),
            pltpu.VMEM((2, NZ, NZ), BF16),
            pltpu.VMEM((2, NX, 2 * NX), BF16),
            pltpu.VMEM((2, NX, 2 * NX), BF16),
            pltpu.VMEM((2, NX, 2 * NX), BF16),
            pltpu.VMEM((8, ATOMS), F32),
            pltpu.VMEM((2, N_DOM, 8, ATOMS), F32),
            pltpu.VMEM((KY, NX, C), F32),
            pltpu.VMEM((2, NX, 2 * NX), BF16),
            pltpu.VMEM((2 * N_DOM, 2, NZ, ATOMS), BF16),
            pltpu.VMEM((2, ROWS + 8, ATOMS), F32),
            pltpu.VMEM((2 * N_DOM, 8, ATOMS), F32),
            pltpu.VMEM((NY // 2, XD * C), F32),
            pltpu.VMEM((NY // 2, XD * C), F32),
            pltpu.VMEM((N_SLAB, XD, KY, C), F32),
            pltpu.VMEM((N_SLAB, XD, KY, C), F32),
            pltpu.VMEM((2, 2 * NX, KY * C), BF16),
            pltpu.VMEM((CHUNKS, N_SLAB, CHUNK, KY, C), F32),
            pltpu.VMEM((CHUNKS, N_SLAB, CHUNK, KY, C), F32),
            pltpu.VMEM((CHUNKS, N_DOM, CHUNK, ROWS, C), F32),
            pltpu.VMEM((CHUNKS, N_DOM, CHUNK, ROWS, C), F32),
            pltpu.VMEM((4, 1, ATOMS), F32),
            pltpu.VMEM((4, 8, ATOMS), F32),
            pltpu.VMEM((4, 8, ATOMS), F32),
            pltpu.SemaphoreType.DMA((5,)),
            pltpu.SemaphoreType.DMA((6,)),
            pltpu.SemaphoreType.DMA,
            pltpu.SemaphoreType.DMA((2, N_DOM)),
            pltpu.SemaphoreType.DMA,
            pltpu.SemaphoreType.DMA((CHUNKS,)),
            pltpu.SemaphoreType.DMA((CHUNKS,)),
            pltpu.SemaphoreType.DMA((4,)),
        ],
        compiler_params=pltpu.CompilerParams(
            collective_id=1, has_side_effects=True, vmem_limit_bytes=53_000_000
        ),
        name="mesh",
    )(
        counts,
        base_cells,
        offsets,
        charges.reshape(1, ATOMS),
        bias_coupling.reshape(1, ATOMS),
        green.transpose(1, 2, 0),
        jnp.asarray(constants()),
    )
    return (potential, gradient.reshape(ATOMS))


def solution(mesh):
    placed = (
        P(None, ("slab", "dom")),
        P(None, ("slab", "dom")),
        P(("slab", "dom")),
        P(("slab", "dom")),
        P(("slab", "dom")),
        P(None, "slab", "dom"),
    )
    return jax.shard_map(
        per_device,
        mesh=mesh,
        in_specs=placed,
        out_specs=(P("slab", "dom", None), P(("slab", "dom"))),
        check_vma=False,
    )
```

time: 114 us -> 95.2 us (0.84)
  Pallas kernels: 103 us -> 88.4 us
  local copies, waits for them, and re-layouts: 7.51 us -> 5.3 us
  other arithmetic: 1.51 us -> 0 us
    pallas_call x1 -> x0, Pallas kernels: 15.8 us -> none  [per_device(): pl.pallas_call(atoms_kernel, out_shape=jax.ShapeDtypeStruct((2, N_DOM, 8,...]
    another operation x2 -> x0, local copies, waits for them, and re-layouts: 1.3 us -> none  [per_device(): jnp.stack([(base_cells[0] % XD).astype(F32), (base_cells[1] % ROWS).astyp...]
    unnamed x15 -> x12, local copies, waits for them, and re-layouts: 6.2 us -> 5.3 us
where the time goes in v1:
time: 95.2 us; the launch traced here: 95 us
  Pallas kernels  88.4 us (93%)
  local copies, waits for them, and re-layouts  5.3 us (6%)
  between operations  1.3 us (1%)
    pallas_call x1, Pallas kernels, per_device(): pl.pallas_call(main_kernel, out_shape=(jax.ShapeDtypeStruct((XD, ROWS, NZ...  88.4 us
    unnamed x12, local copies, waits for them, and re-layouts  5.3 us

profile of v1, /device:TPU:1, one launch (start us, length us, event | category | flops | bytes accessed | tf_op | source)
XLA Modules:
  0.0 95.0 jit_solution(10756279174271686757)
XLA Ops:
  1.3 0.0 copy-start
  1.3 1.0 %copy-done = f32[256,8,64]{0,2,1:T(8,128)S(1)} copy-done((f32[256,8,64]{0,2,1:T(8,128)S(1)}, f32[256,8,64]{0,2,1:T(8,128)}, u32[]{:S(2)}) %copy-start) | copy-done | bytes 524312
  2.3 0.0 copy-start.1
  2.3 0.7 copy-done.1
  3.0 0.0 copy-start.2
  3.0 0.7 copy-done.2
  3.7 0.0 copy-start.3
  3.7 0.7 copy-done.3
  4.4 0.0 copy-start.4
  4.4 0.7 copy-done.4
  5.1 88.4 %mesh.1 = (f32[4,128,512]{2,1,0:T(8,128)S(1)}, f32[1,256]{1,0:T(1,128)S(1)}) custom-call(s32[1]{0:T(128)S(6)} %copy.11.counts_ref, s32[3,256]{1,0:T(4,128)S(1)} %copy-done.1, f32[3,256]{1,0:T(4,128)S(1)} %copy-done.2, f32[1,256]{1,0:T(1,128)S(1)} %bitcast.5, f32[1,256]{1,0:T(1,128)S(1)} %bitcast.6, f32[8,64,256]{2,1,0:T(8,128)S(1)} %bitcast.4, ...), custom_call_target="tpu_custom_call" | custom-call | tf_op jit(solution)/shard_map/mesh/pallas_call | solution.py:381
  93.4 1.0 %copy.12 = f32[4,128,512]{2,1,0:T(8,128)} copy(f32[4,128,512]{2,1,0:T(8,128)S(1)} %get-tuple-element.8) | data formatting | bytes 2097152
  94.4 0.6 copy.13
Async XLA Ops:
  1.3 1.0 %copy-start = (f32[256,8,64]{0,2,1:T(8,128)S(1)}, f32[256,8,64]{0,2,1:T(8,128)}, u32[]{:S(2)}) copy-start(f32[256,8,64]{0,2,1:T(8,128)} %param.12) | copy-start | bytes 1572868
  2.3 0.7 copy-start.1
  3.0 0.7 copy-start.2
  3.7 0.7 copy-start.3
  4.4 0.7 copy-start.4

commit v2 on v1

--- a/solution.py
+++ b/solution.py
@@ -45,7 +45,12 @@
     cs_even = np.concatenate([np.cos(even), np.sin(even)], 1)
     cs_odd = np.concatenate([np.cos(odd), np.sin(odd)], 1)
     cs_odd_t = np.concatenate([np.cos(odd).T, np.sin(odd).T], 1)
-    return halves(np.concatenate([fz, cs_even, cs_odd, cs_odd_t], 0))
+    main = halves(np.concatenate([fz, cs_even, cs_odd, cs_odd_t], 0))
+    coarse, fine = halves(fz[:, ::16]), halves(fz[:, :32])
+    blank = np.zeros((NZ, 64), jnp.bfloat16)
+    pair = np.concatenate([coarse[0], coarse[1], blank, fine[0], fine[0], fine[1], blank[:, :32]], 1)
+    pair = pair.reshape(2, 2, C, 256).transpose(0, 2, 1, 3).reshape(2, C, 512)
+    return np.concatenate([main, pair], 1)
 
 
 def split(value):
@@ -101,18 +106,28 @@
     return ((z + dz) % 8) * 8 + ((y + dy) % 4) * 2 + (c + dc) % 2
 
 
+FAR = N_SLAB // 2
+SENDS = ((0, 0, 0), (0, 1, 1), (1, 0, FAR), (1, 1, FAR + 1))
+AWAY = (0, 1, N_SLAB - 1, FAR, FAR + 1, FAR - 1)
+
+
+def near_plane(z, m):
+    first = z + 7 - z % 2
+    return (first + (m + 64 - first) % 4) % 8
+
+
 def signal(target):
     pl.semaphore_signal(pltpu.get_barrier_semaphore(), inc=1, device_id=target, device_id_type=MESH)
 
 
 def main_kernel(
-    counts_ref, cells_ref, offsets_ref, charges_ref, bias_ref, green_hbm, table_hbm,
-    pot_ref, grad_ref,
-    green, fz, even_m, odd_m, back_odd,
+    counts_ref, cells_ref, offsets_ref, charges_ref, green_hbm, table_hbm,
+    pot_hbm, grad_ref,
+    green, fz, even_m, odd_m, back_odd, phases,
     own_ref, atoms_ref, factors, by_plane,
     hot_z, wy_tab, wx_tab, grid_even, grid_odd, send1, recv1, spectrum, send2, recv2, send3, recv3,
-    totals, parts, parts_in,
-    load_sem, send_sem, atom_send, atom_recv, r1, r2, r3, r4,
+    pot_ref, totals, parts, parts_in,
+    load_sem, pot_sem, send_sem, atom_send, atom_recv, r1, r2, r3, r4,
 ):
     s, d = lax.axis_index("slab"), lax.axis_index("dom")
     nxt, prv = (s + 1) % N_SLAB, (s + N_SLAB - 1) % N_SLAB
@@ -123,9 +138,8 @@
         return carry
 
     for i in range(1, N_DOM):
-        signal((s, (d + i) % N_DOM))
-        signal((nxt, (d + i) % N_DOM))
-        signal((prv, (d + i) % N_DOM))
+        for step in AWAY:
+            signal(((s + step) % N_SLAB, (d + i) % N_DOM))
     lax.fori_loop(1, N_SLAB, greet, 0)
 
     loads = [
@@ -137,6 +151,10 @@
                 (table_hbm.at[:, NZ + NX : NZ + 2 * NX], odd_m),
                 (green_hbm, green),
                 (table_hbm.at[:, NZ + 2 * NX : NZ + 3 * NX], back_odd),
+                (
+                    table_hbm.at[d // 2, pl.ds(NZ + 3 * NX, C), pl.ds(pl.multiple_of((d % 2) * 256, 256), 256)],
+                    phases,
+                ),
             ]
         )
     ]
@@ -151,7 +169,7 @@
     own_ref[3:6] = offsets_ref[...]
     own_ref[6:7] = jnp.where(alive, charges_ref[...], 0.0)
     own_ref[7:8] = jnp.zeros((1, ATOMS), F32)
-    atoms_ref[0, d] = own_ref[...]
+    atoms_ref[0, 0, d] = own_ref[...]
     grid_even[...] = jnp.zeros_like(grid_even)
     grid_odd[...] = jnp.zeros_like(grid_odd)
     totals[...] = jnp.zeros_like(totals)
@@ -168,7 +186,7 @@
     loads[3].wait()
     lane = lax.broadcasted_iota(jnp.int32, (1, C), 1)
     zero_bin = jnp.logical_and(lane % (C // 2) == 0, d == 0)
-    scale = jnp.where(zero_bin, 1.0, 2.0).astype(F32) * (1.0 / (NX * NY * NZ))
+    scale = jnp.where(zero_bin, 1.0, 2.0).astype(F32)
 
     def prepare(t, carry):
         f = green[t]
@@ -177,22 +195,23 @@
 
     lax.fori_loop(0, KY, prepare, 0)
 
-    pl.semaphore_wait(pltpu.get_barrier_semaphore(), N_SLAB - 1 + 3 * (N_DOM - 1))
-
-    for g in range(2):
+    pl.semaphore_wait(pltpu.get_barrier_semaphore(), N_SLAB - 1 + len(AWAY) * (N_DOM - 1))
+
+    for h, g, step in SENDS:
         for i in range(N_DOM):
-            if i == 0 and g == 0:
+            if h == g == i == 0:
                 continue
             pltpu.make_async_remote_copy(
                 own_ref,
-                atoms_ref.at[g, d],
+                atoms_ref.at[h, g, d],
                 atom_send,
-                atom_recv.at[g, i],
-                device_id=(nxt if g else s, (d + i) % N_DOM),
+                atom_recv.at[h, g, i],
+                device_id=((s + step) % N_SLAB, (d + i) % N_DOM),
                 device_id_type=MESH,
             ).start()
 
-    row_z = lax.broadcasted_iota(jnp.int32, (NZ, ATOMS), 0)
+    row_h = lax.broadcasted_iota(jnp.int32, (64, ATOMS), 0) % 32
+    row_l = lax.broadcasted_iota(jnp.int32, (32, ATOMS), 0)
     row = lax.broadcasted_iota(jnp.int32, (ROWS + EXTRA, ATOMS), 0)
     half = ROWS // 2
     row_y = jnp.where(
@@ -201,68 +220,95 @@
         ROWS + 2 * ((row - ROWS) % (EXTRA // 2)) + (row - ROWS) // (EXTRA // 2),
     )
     row_x = lax.broadcasted_iota(jnp.int32, (8, ATOMS), 0)
-    loads[0].wait()
-    mine = pl.ds(pl.multiple_of(d * C, C), C)
-    fz_mine = (fz[0, mine], fz[1, mine])
-
-    def spread(n, carry):
-        i, g = n // 2, n % 2
+    loads[5].wait()
+
+    z, inner = s // 8, s % 8
+    served = near_plane(z, lax.broadcasted_iota(jnp.int32, (NX, 2 * C), 0) // 64)
+    sign = jnp.where(served < 4, 1.0, -1.0).astype(F32)
+    here = (z % 4) * 8 + inner
+    loads[2].wait()
+
+    def spread(i, h):
         e = (d + i) % N_DOM
-
-        @pl.when(n > 0)
-        def _():
-            block = atoms_ref.at[g, e]
-            pltpu.make_async_copy(block, block, atom_recv.at[g, (N_DOM - i) % N_DOM]).wait()
-
-        data = atoms_ref[g, e]
-        whole = data[0:3].astype(jnp.int32)
-        hz = split(hot((row_z - whole[2:3]) & (NZ - 1), spline_rows(data[5:6])))
-        hot_z[n, 0] = hz[0]
-        hot_z[n, 1] = hz[1]
-        wx = hot(row_x - whole[0:1] + XD * g, spline_rows(data[3:4]))
-        wx_tab[n] = wx
-        wy = hot(row_y - whole[1:2], spline_rows(data[4:5]))
-        lines = dot3(fz_mine, hz) * data[6:7]
-        scaled = split(jnp.concatenate([lines * wx[p : p + 1] for p in range(XD)], 0))
-        out = dot3(split(wy), scaled, NT)
-        here = pl.ds(pl.multiple_of(e * half, half), half)
+        rows_y, scaled = [], []
+        for g in range(2):
+
+            def arrive():
+                block = atoms_ref.at[h, g, e]
+                pltpu.make_async_copy(block, block, atom_recv.at[h, g, (N_DOM - i) % N_DOM]).wait()
+
+            if g == 0:
+                pl.when(h + i > 0)(arrive)
+            else:
+                arrive()
+            data = atoms_ref[h, g, e]
+            whole = data[0:3].astype(jnp.int32)
+            cell = whole[2:3]
+            coarse = jnp.where(row_h == cell // 16, 1.0, 0.0).astype(BF16)
+            fine = split(hot(row_l - cell % 16, spline_rows(data[5:6])))
+            a = jnp.dot(phases[:, :64], coarse, preferred_element_type=F32)
+            b = jnp.dot(
+                phases[:, C : C + 96],
+                jnp.concatenate([fine[0], fine[1], fine[0]], 0),
+                preferred_element_type=F32,
+            )
+            a_re, a_im, b_re, b_im = a[: C // 2], a[C // 2 :], b[: C // 2], b[C // 2 :]
+            lines = jnp.concatenate([a_re * b_re - a_im * b_im, a_re * b_im + a_im * b_re], 0) * data[6:7]
+            wx = hot(row_x - whole[0:1] + XD * g, spline_rows(data[3:4]))
+            rows_y.append(hot(row_y - whole[1:2], spline_rows(data[4:5])))
+            scaled.append(jnp.concatenate([lines * wx[p : p + 1] for p in range(XD)], 0))
+        out = dot3(split(jnp.concatenate(rows_y, 1)), split(jnp.concatenate(scaled, 1)), NT)
+        own_rows = pl.ds(pl.multiple_of(e * half, half), half)
         after = pl.ds(pl.multiple_of(((e + 1) % N_DOM) * half, half), EXTRA // 2)
-        grid_even[here, :] += out[:half]
-        grid_odd[here, :] += out[half:ROWS]
-        grid_even[after, :] += out[ROWS : ROWS + EXTRA // 2]
-        grid_odd[after, :] += out[ROWS + EXTRA // 2 :]
+        grid_even[h, own_rows, :] += out[:half]
+        grid_odd[h, own_rows, :] += out[half:ROWS]
+        grid_even[h, after, :] += out[ROWS : ROWS + EXTRA // 2]
+        grid_odd[h, after, :] += out[ROWS + EXTRA // 2 :]
+        return h
+
+    def outward(h, carry):
+        lax.fori_loop(0, N_DOM, spread, h)
+        for pair in range(2):
+            lanes = slice(2 * C * pair, 2 * C * (pair + 1))
+            a = dot3((even_m[0], even_m[1]), stacked(grid_even[h, :, lanes], 1.0))
+            b = dot3((odd_m[0], odd_m[1]), stacked(grid_odd[h, :, lanes], 1.0))
+            value = a + sign * b
+            for q in range(2):
+                send1[:, h, 2 * pair + q] = value[:, C * q : C * (q + 1)].reshape(FAR, KY, C)
+
+        def post1(k, inside):
+            j = (here + k) % FAR
+            t = near_plane(z, j // 8) * 8 + j % 8
+            pltpu.make_async_remote_copy(
+                send1.at[j, h],
+                recv1.at[(s + FAR * h) % N_SLAB],
+                send_sem.at[0],
+                r1,
+                device_id=(t, d),
+                device_id_type=MESH,
+            ).start()
+            return inside
+
+        lax.fori_loop(1, FAR, post1, 0)
         return carry
 
-    lax.fori_loop(0, 2 * N_DOM, spread, 0)
-
-    loads[2].wait()
-    for pair in range(2):
-        lanes = slice(2 * C * pair, 2 * C * (pair + 1))
-        a = dot3((even_m[0], even_m[1]), stacked(grid_even[:, lanes], 1.0))
-        b = dot3((odd_m[0], odd_m[1]), stacked(grid_odd[:, lanes], 1.0))
-        for first, value in ((0, a + b), (N_SLAB // 2, a - b)):
-            for q in range(2):
-                send1[first : first + N_SLAB // 2, 2 * pair + q] = value[:, C * q : C * (q + 1)].reshape(
-                    N_SLAB // 2, KY, C
-                )
-
-    def post1(k, carry):
-        t = shifted_slab(s, k)
-        pltpu.make_async_remote_copy(
-            send1.at[t], recv1.at[s], send_sem.at[0], r1, device_id=(t, d), device_id_type=MESH
-        ).start()
-        return carry
-
-    lax.fori_loop(1, N_SLAB, post1, 0)
+    lax.fori_loop(0, 2, outward, 0)
+    for h in range(2):
+        recv1[(s + FAR * h) % N_SLAB] = send1[here, h]
     natural = lax.broadcasted_iota(jnp.int32, (ROWS, ATOMS), 0)
+    row_z = lax.broadcasted_iota(jnp.int32, (NZ, ATOMS), 0)
     for g in range(2):
-        for first, size, e in ((0, ROWS, d), (ROWS, 8, left)):
-            data = atoms_ref[g, e]
-            base = data[1:2].astype(jnp.int32)
-            wy_tab[g, first : first + size] = hot(first + natural[:size] - base, spline_rows(data[4:5]))
-    recv1[s] = send1[s]
+        for n, first, size, e in ((0, 0, ROWS, d), (1, ROWS, 8, left)):
+            data = atoms_ref[0, g, e]
+            whole = data[0:3].astype(jnp.int32)
+            wy_tab[g, first : first + size] = hot(first + natural[:size] - whole[1:2], spline_rows(data[4:5]))
+            wx_tab[2 * n + g] = hot(row_x - whole[0:1] + XD * g, spline_rows(data[3:4]))
+            hz = split(hot((row_z - whole[2:3]) & (NZ - 1), spline_rows(data[5:6])))
+            hot_z[2 * n + g, 0] = hz[0]
+            hot_z[2 * n + g, 1] = hz[1]
     others = pl.ds(0, N_SLAB - 1)
-    pltpu.make_async_copy(recv1.at[others], recv1.at[others], r1).wait()
+    sent1 = pl.ds(0, N_SLAB - 2)
+    pltpu.make_async_copy(recv1.at[sent1], recv1.at[sent1], r1).wait()
 
     flat1 = recv1.reshape(NX * KY, C)
     for pair in range(KY // 2):
@@ -298,6 +344,7 @@
         return carry
 
     lax.fori_loop(0, CHUNKS, along_x, 0)
+    loads[0].wait()
     loads[4].wait()
     three = pl.ds(0, N_DOM - 1)
 
@@ -334,17 +381,19 @@
             block = dot3(split(columns), (fz[0], fz[1]))
             for q in range(CHUNK):
                 pot_ref[CHUNK * c + q] = block[q * ROWS : (q + 1) * ROWS]
+            done = pl.ds(pl.multiple_of(CHUNK * c, CHUNK), CHUNK)
+            pltpu.make_async_copy(pot_ref.at[done], pot_hbm.at[done], pot_sem).start()
             both = split(block)
             edge = split(jnp.concatenate([block[q * ROWS : q * ROWS + 8] for q in range(CHUNK)], 0))
             for g in range(2):
                 u = dot3(both, (hot_z[g, 0], hot_z[g, 1]))
-                v = dot3(edge, (hot_z[6 + g, 0], hot_z[6 + g, 1]))
+                v = dot3(edge, (hot_z[2 + g, 0], hot_z[2 + g, 1]))
                 for q in range(CHUNK):
                     p = CHUNK * c + q
                     here = jnp.sum(u[q * ROWS : (q + 1) * ROWS] * wy_tab[g, :ROWS], 0, keepdims=True)
                     there = jnp.sum(v[q * 8 : (q + 1) * 8] * wy_tab[g, ROWS:], 0, keepdims=True)
                     totals[2 * g] += here * wx_tab[g, pl.ds(p, 1)]
-                    totals[2 * g + 1] += there * wx_tab[6 + g, pl.ds(p, 1)]
+                    totals[2 * g + 1] += there * wx_tab[2 + g, pl.ds(p, 1)]
 
         return carry
 
@@ -359,11 +408,12 @@
     for n in range(1, 4):
         pltpu.make_async_copy(parts_in.at[n], parts_in.at[n], r4.at[n]).wait()
     total = totals[0] + parts_in[1, 0:1] + parts_in[2, 0:1] + parts_in[3, 0:1]
-    grad_ref[...] = jnp.where(alive, bias_ref[...] * total, 0.0)
-
-    seven = atoms_ref.reshape(2 * N_DOM, 8, ATOMS).at[pl.ds(0, 2 * N_DOM - 1)]
-    pltpu.make_async_copy(seven, seven, atom_send).wait()
-    pltpu.make_async_copy(send1.at[others], send1.at[others], send_sem.at[0]).wait()
+    grad_ref[...] = total
+    pltpu.make_async_copy(pot_ref, pot_hbm, pot_sem).wait()
+
+    gone = atoms_ref.reshape(4 * N_DOM, 8, ATOMS).at[pl.ds(0, 4 * N_DOM - 1)]
+    pltpu.make_async_copy(gone, gone, atom_send).wait()
+    pltpu.make_async_copy(recv1.at[sent1], recv1.at[sent1], send_sem.at[0]).wait()
 
     def drain(ch, carry):
         pltpu.make_async_copy(send2.at[ch, others], send2.at[ch, others], send_sem.at[1]).wait()
@@ -384,44 +434,47 @@
             jax.ShapeDtypeStruct((XD, ROWS, NZ), F32),
             jax.ShapeDtypeStruct((1, ATOMS), F32),
         ),
-        in_specs=[pl.BlockSpec(memory_space=pltpu.SMEM)] + [vmem] * 4 + [hbm] * 2,
-        out_specs=(vmem, vmem),
+        in_specs=[pl.BlockSpec(memory_space=pltpu.SMEM)] + [vmem] * 3 + [hbm] * 2,
+        out_specs=(hbm, vmem),
         scratch_shapes=[
             pltpu.VMEM((KY, C // 2, NX), F32),
             pltpu.VMEM((2, NZ, NZ), BF16),
             pltpu.VMEM((2, NX, 2 * NX), BF16),
             pltpu.VMEM((2, NX, 2 * NX), BF16),
             pltpu.VMEM((2, NX, 2 * NX), BF16),
+            pltpu.VMEM((C, 256), BF16),
             pltpu.VMEM((8, ATOMS), F32),
-            pltpu.VMEM((2, N_DOM, 8, ATOMS), F32),
+            pltpu.VMEM((2, 2, N_DOM, 8, ATOMS), F32),
             pltpu.VMEM((KY, NX, C), F32),
             pltpu.VMEM((2, NX, 2 * NX), BF16),
-            pltpu.VMEM((2 * N_DOM, 2, NZ, ATOMS), BF16),
+            pltpu.VMEM((4, 2, NZ, ATOMS), BF16),
             pltpu.VMEM((2, ROWS + 8, ATOMS), F32),
-            pltpu.VMEM((2 * N_DOM, 8, ATOMS), F32),
-            pltpu.VMEM((NY // 2, XD * C), F32),
-            pltpu.VMEM((NY // 2, XD * C), F32),
-            pltpu.VMEM((N_SLAB, XD, KY, C), F32),
+            pltpu.VMEM((4, 8, ATOMS), F32),
+            pltpu.VMEM((2, NY // 2, XD * C), F32),
+            pltpu.VMEM((2, NY // 2, XD * C), F32),
+            pltpu.VMEM((FAR, 2, XD, KY, C), F32),
             pltpu.VMEM((N_SLAB, XD, KY, C), F32),
             pltpu.VMEM((2, 2 * NX, KY * C), BF16),
             pltpu.VMEM((CHUNKS, N_SLAB, CHUNK, KY, C), F32),
             pltpu.VMEM((CHUNKS, N_SLAB, CHUNK, KY, C), F32),
             pltpu.VMEM((CHUNKS, N_DOM, CHUNK, ROWS, C), F32),
             pltpu.VMEM((CHUNKS, N_DOM, CHUNK, ROWS, C), F32),
+            pltpu.VMEM((XD, ROWS, NZ), F32),
             pltpu.VMEM((4, 1, ATOMS), F32),
             pltpu.VMEM((4, 8, ATOMS), F32),
             pltpu.VMEM((4, 8, ATOMS), F32),
-            pltpu.SemaphoreType.DMA((5,)),
             pltpu.SemaphoreType.DMA((6,)),
             pltpu.SemaphoreType.DMA,
-            pltpu.SemaphoreType.DMA((2, N_DOM)),
+            pltpu.SemaphoreType.DMA((6,)),
+            pltpu.SemaphoreType.DMA,
+            pltpu.SemaphoreType.DMA((2, 2, N_DOM)),
             pltpu.SemaphoreType.DMA,
             pltpu.SemaphoreType.DMA((CHUNKS,)),
             pltpu.SemaphoreType.DMA((CHUNKS,)),
             pltpu.SemaphoreType.DMA((4,)),
         ],
         compiler_params=pltpu.CompilerParams(
-            collective_id=1, has_side_effects=True, vmem_limit_bytes=53_000_000
+            collective_id=1, has_side_effects=True, vmem_limit_bytes=64_500_000
         ),
         name="mesh",
     )(
@@ -429,11 +482,13 @@
         base_cells,
         offsets,
         charges.reshape(1, ATOMS),
-        bias_coupling.reshape(1, ATOMS),
         green.transpose(1, 2, 0),
         jnp.asarray(constants()),
     )
-    return (potential, gradient.reshape(ATOMS))
+    norm = 1.0 / (NX * NY * NZ)
+    alive = jnp.arange(ATOMS, dtype=jnp.int32) < counts[0]
+    gradient = jnp.where(alive, bias_coupling * (gradient.reshape(ATOMS) * norm), 0.0)
+    return (potential * norm, gradient)
 
 
 def solution(mesh):

time: 95.2 us -> 81.9 us (0.86)
  Pallas kernels: 88.4 us -> 76.9 us
  local copies, waits for them, and re-layouts: 5.3 us -> 0.01 us
  other arithmetic: 0 us -> 3.54 us
    pallas_call x1, Pallas kernels: 88.4 us -> 76.9 us  [per_device(): pl.pallas_call(main_kernel, out_shape=(jax.ShapeDtypeStruct((XD, ROWS, NZ...]
    unnamed x12 -> x2, local copies, waits for them, and re-layouts: 5.3 us -> 0.01 us
    mul x0 -> x2, other arithmetic: none -> 2.97 us  [the longest x1 2.31 us: per_device(): return (potential * norm, gradient)]
where the time goes in v2:
time: 81.9 us; the launch traced here: 81.7 us
  Pallas kernels  76.9 us (94%)
  other arithmetic  3.54 us (4%)
  between operations  1.31 us (2%)
    pallas_call x1, Pallas kernels, per_device(): pl.pallas_call(main_kernel, out_shape=(jax.ShapeDtypeStruct((XD, ROWS, NZ...  76.9 us
    mul x1, other arithmetic, per_device(): return (potential * norm, gradient)  2.31 us

profile of v2, /device:TPU:1, one launch (start us, length us, event | category | flops | bytes accessed | tf_op | source)
XLA Modules:
  0.0 81.7 jit_solution(3656394297502697819)
XLA Ops:
  0.6 0.0 copy-start
  1.3 76.9 %mesh.1 = (f32[4,128,512]{2,1,0:T(8,128)}, f32[1,256]{1,0:T(1,128)}) custom-call(s32[1]{0:T(128)} %copy.9.counts_ref, s32[3,256]{1,0:T(4,128)} %cells_ref.1, f32[3,256]{1,0:T(4,128)} %offsets_ref.1, f32[1,256]{1,0:T(1,128)} %bitcast.7, f32[8,64,256]{2,1,0:T(8,128)} %bitcast.5, bf16[2,1408,512]{2,1,0:T(8,128)(2,1)} %constant.2.clone.table_hbm), custom_call_target="tpu_custom_call" | custom-call | tf_op jit(solution)/shard_map/mesh/pallas_call | solution.py:431
  78.2 0.7 broadcast_multiply_fusion.1
  78.8 0.0 copy-done
  78.8 0.6 compare_select_fusion
  79.4 2.3 %broadcast_multiply_fusion = f32[4,128,512]{2,1,0:T(8,128)} fusion(f32[4,128,512]{2,1,0:T(8,128)} %get-tuple-element.4), kind=kLoop, calls=%fused_computation | loop fusion | flops 262144 | bytes 2097152 | tf_op jit(solution)/shard_map/mul | solution.py:491
Async XLA Ops:
  0.6 78.2 %copy-start = (f32[256]{0:T(256)S(1)}, f32[256]{0:T(256)}, u32[]{:S(2)}) copy-start(f32[256]{0:T(256)} %param.10) | copy-start | bytes 3076

commit v3 on v2

--- a/solution.py
+++ b/solution.py
@@ -162,7 +162,7 @@
         load.start()
 
     slot = lax.broadcasted_iota(jnp.int32, (1, ATOMS), 1)
-    alive = slot < counts_ref[0]
+    alive = slot < counts_ref[...]
     own_ref[0:1] = (cells_ref[0:1] % XD).astype(F32)
     own_ref[1:2] = (cells_ref[1:2] % ROWS).astype(F32)
     own_ref[2:3] = cells_ref[2:3].astype(F32)
@@ -277,7 +277,7 @@
                 send1[:, h, 2 * pair + q] = value[:, C * q : C * (q + 1)].reshape(FAR, KY, C)
 
         def post1(k, inside):
-            j = (here + k) % FAR
+            j = (here + 13 * k) % FAR
             t = near_plane(z, j // 8) * 8 + j % 8
             pltpu.make_async_remote_copy(
                 send1.at[j, h],
@@ -328,7 +328,7 @@
             flat2[ch, pl.ds(t, per, stride=KY), :] = out[:, C * t : C * (t + 1)]
 
         def post2(k, inner):
-            t = shifted_slab(s, k)
+            t = shifted_slab(s, (29 * k) % N_SLAB)
             pltpu.make_async_remote_copy(
                 send2.at[ch, t],
                 recv2.at[ch, s],
@@ -347,6 +347,13 @@
     loads[0].wait()
     loads[4].wait()
     three = pl.ds(0, N_DOM - 1)
+
+    def deliver(n):
+        target = ((s, left), (prv, d), (prv, left))[n - 1]
+        parts[n] = jnp.broadcast_to(totals[n], (8, ATOMS))
+        pltpu.make_async_remote_copy(
+            parts.at[n], parts_in.at[n], send_sem.at[2 + n], r4.at[n], device_id=target, device_id_type=MESH
+        ).start()
 
     def finish(ch, carry):
         @pl.when(ch < CHUNKS)
@@ -385,7 +392,8 @@
             pltpu.make_async_copy(pot_ref.at[done], pot_hbm.at[done], pot_sem).start()
             both = split(block)
             edge = split(jnp.concatenate([block[q * ROWS : q * ROWS + 8] for q in range(CHUNK)], 0))
-            for g in range(2):
+
+            def sample(g):
                 u = dot3(both, (hot_z[g, 0], hot_z[g, 1]))
                 v = dot3(edge, (hot_z[2 + g, 0], hot_z[2 + g, 1]))
                 for q in range(CHUNK):
@@ -395,20 +403,26 @@
                     totals[2 * g] += here * wx_tab[g, pl.ds(p, 1)]
                     totals[2 * g + 1] += there * wx_tab[2 + g, pl.ds(p, 1)]
 
+            sample(0)
+
+            @pl.when(c < CHUNKS - 1)
+            def _():
+                sample(1)
+
+            @pl.when(c == CHUNKS - 2)
+            def _():
+                deliver(2)
+                deliver(3)
+
         return carry
 
     lax.fori_loop(0, CHUNKS + 1, finish, 0)
 
-    for n in range(1, 4):
-        parts[n] = jnp.broadcast_to(totals[n], (8, ATOMS))
-    for n, target in ((1, (s, left)), (2, (prv, d)), (3, (prv, left))):
-        pltpu.make_async_remote_copy(
-            parts.at[n], parts_in.at[n], send_sem.at[2 + n], r4.at[n], device_id=target, device_id_type=MESH
-        ).start()
+    deliver(1)
     for n in range(1, 4):
         pltpu.make_async_copy(parts_in.at[n], parts_in.at[n], r4.at[n]).wait()
     total = totals[0] + parts_in[1, 0:1] + parts_in[2, 0:1] + parts_in[3, 0:1]
-    grad_ref[...] = total
+    grad_ref[...] = total * (1.0 / (NX * NY * NZ))
     pltpu.make_async_copy(pot_ref, pot_hbm, pot_sem).wait()
 
     gone = atoms_ref.reshape(4 * N_DOM, 8, ATOMS).at[pl.ds(0, 4 * N_DOM - 1)]
@@ -434,7 +448,7 @@
             jax.ShapeDtypeStruct((XD, ROWS, NZ), F32),
             jax.ShapeDtypeStruct((1, ATOMS), F32),
         ),
-        in_specs=[pl.BlockSpec(memory_space=pltpu.SMEM)] + [vmem] * 3 + [hbm] * 2,
+        in_specs=[vmem] * 4 + [hbm] * 2,
         out_specs=(hbm, vmem),
         scratch_shapes=[
             pltpu.VMEM((KY, C // 2, NX), F32),
@@ -478,7 +492,7 @@
         ),
         name="mesh",
     )(
-        counts,
+        counts.reshape(1, 1),
         base_cells,
         offsets,
         charges.reshape(1, ATOMS),
@@ -487,7 +501,7 @@
     )
     norm = 1.0 / (NX * NY * NZ)
     alive = jnp.arange(ATOMS, dtype=jnp.int32) < counts[0]
-    gradient = jnp.where(alive, bias_coupling * (gradient.reshape(ATOMS) * norm), 0.0)
+    gradient = jnp.where(alive, bias_coupling * gradient.reshape(ATOMS), 0.0)
     return (potential * norm, gradient)
 
 

time: 81.9 us -> 79.9 us (0.976); the launches traced: 81.7 us -> 78.9 us
  Pallas kernels: 76.9 us -> 74 us
    pallas_call x1, Pallas kernels: 76.9 us -> 74 us  [per_device(): pl.pallas_call(main_kernel, out_shape=(jax.ShapeDtypeStruct((XD, ROWS, NZ...]
where the time goes in v3:
time: 79.9 us; the launch traced here: 78.9 us
  Pallas kernels  74 us (93%)
  other arithmetic  3.53 us (4%)
  between operations  1.32 us (2%)
    pallas_call x1, Pallas kernels, per_device(): pl.pallas_call(main_kernel, out_shape=(jax.ShapeDtypeStruct((XD, ROWS, NZ...  74 us
    mul x1, other arithmetic, per_device(): return (potential * norm, gradient)  2.31 us

profile of v3, /device:TPU:1, one launch (start us, length us, event | category | flops | bytes accessed | tf_op | source)
XLA Modules:
  0.0 78.9 jit_solution(4037876193366788637)
XLA Ops:
  0.6 0.0 copy-start
  1.3 74.0 %mesh.1 = (f32[4,128,512]{2,1,0:T(8,128)}, f32[1,256]{1,0:T(1,128)}) custom-call(s32[1,1]{1,0:T(1,128)} %bitcast.5.counts_ref, s32[3,256]{1,0:T(4,128)} %cells_ref.1, f32[3,256]{1,0:T(4,128)} %offsets_ref.1, f32[1,256]{1,0:T(1,128)} %bitcast.8, f32[8,64,256]{2,1,0:T(8,128)} %bitcast.7, bf16[2,1408,512]{2,1,0:T(8,128)(2,1)} %constant.6.clone.table_hbm), custom_call_target="tpu_custom_call" | custom-call | tf_op jit(solution)/shard_map/mesh/pallas_call | solution.py:445
  75.3 0.0 copy-done
  75.4 1.2 %compare_select_fusion = f32[256]{0:T(256)} fusion(f32[256]{0:T(256)S(1)} %copy-done, f32[256]{0:T(256)} %bitcast.9, s32[]{:T(128)} %bitcast.6), kind=kLoop, calls=%fused_computation.1 | loop fusion | flops 768 | bytes 3076 | tf_op jit(solution)/shard_map/jit(_where)/select_n | solution.py:504
  76.6 2.3 %broadcast_multiply_fusion = f32[4,128,512]{2,1,0:T(8,128)} fusion(f32[4,128,512]{2,1,0:T(8,128)} %get-tuple-element.4), kind=kLoop, calls=%fused_computation | loop fusion | flops 262144 | bytes 2097152 | tf_op jit(solution)/shard_map/mul | solution.py:505
Async XLA Ops:
  0.6 74.7 %copy-start = (f32[256]{0:T(256)S(1)}, f32[256]{0:T(256)}, u32[]{:S(2)}) copy-start(f32[256]{0:T(256)} %param.10) | copy-start | bytes 3076

commit v4 on v3

--- a/solution.py
+++ b/solution.py
@@ -422,7 +422,7 @@
     for n in range(1, 4):
         pltpu.make_async_copy(parts_in.at[n], parts_in.at[n], r4.at[n]).wait()
     total = totals[0] + parts_in[1, 0:1] + parts_in[2, 0:1] + parts_in[3, 0:1]
-    grad_ref[...] = total * (1.0 / (NX * NY * NZ))
+    grad_ref[...] = jnp.where(alive, total * (1.0 / (NX * NY * NZ)), 0.0)
     pltpu.make_async_copy(pot_ref, pot_hbm, pot_sem).wait()
 
     gone = atoms_ref.reshape(4 * N_DOM, 8, ATOMS).at[pl.ds(0, 4 * N_DOM - 1)]
@@ -500,8 +500,7 @@
         jnp.asarray(constants()),
     )
     norm = 1.0 / (NX * NY * NZ)
-    alive = jnp.arange(ATOMS, dtype=jnp.int32) < counts[0]
-    gradient = jnp.where(alive, bias_coupling * gradient.reshape(ATOMS), 0.0)
+    gradient = bias_coupling * gradient.reshape(ATOMS)
     return (potential * norm, gradient)
 
 

time: 79.9 us -> 80 us (level)
    select_n x1 -> x0, other arithmetic: 1.22 us -> none  [per_device(): gradient = jnp.where(alive, bias_coupling * gradient.reshape(ATOMS), 0.0)]
    mul x0 -> x1, other arithmetic: none -> 1.22 us  [per_device(): gradient = bias_coupling * gradient.reshape(ATOMS)]
where the time goes in v4:
time: 80 us; the launch traced here: 78.9 us
  Pallas kernels  74.1 us (93%)
  other arithmetic  3.53 us (4%)
  between operations  1.31 us (2%)
    pallas_call x1, Pallas kernels, per_device(): pl.pallas_call(main_kernel, out_shape=(jax.ShapeDtypeStruct((XD, ROWS, NZ...  74.1 us
    mul x1, other arithmetic, per_device(): return (potential * norm, gradient)  2.31 us

profile of v4, /device:TPU:1, one launch (start us, length us, event | category | flops | bytes accessed | tf_op | source)
XLA Modules:
  0.0 78.9 jit_solution(17087619182436713159)
XLA Ops:
  0.6 0.0 copy-start
  1.3 74.1 %mesh.1 = (f32[4,128,512]{2,1,0:T(8,128)}, f32[1,256]{1,0:T(1,128)}) custom-call(s32[1,1]{1,0:T(1,128)} %bitcast.4.counts_ref, s32[3,256]{1,0:T(4,128)} %cells_ref.1, f32[3,256]{1,0:T(4,128)} %offsets_ref.1, f32[1,256]{1,0:T(1,128)} %bitcast.6, f32[8,64,256]{2,1,0:T(8,128)} %bitcast.5, bf16[2,1408,512]{2,1,0:T(8,128)(2,1)} %constant.4.clone.table_hbm), custom_call_target="tpu_custom_call" | custom-call | tf_op jit(solution)/shard_map/mesh/pallas_call | solution.py:445
  75.4 2.3 %broadcast_multiply_fusion = f32[4,128,512]{2,1,0:T(8,128)} fusion(f32[4,128,512]{2,1,0:T(8,128)} %get-tuple-element.4), kind=kLoop, calls=%fused_computation | loop fusion | flops 262144 | bytes 2097152 | tf_op jit(solution)/shard_map/mul | solution.py:504
  77.7 0.0 copy-done
  77.7 1.2 %mul.11 = f32[256]{0:T(256)} multiply(f32[256]{0:T(256)S(1)} %copy-done, f32[256]{0:T(256)} %bitcast.7) | non-fusion elementwise | flops 256 | bytes 3072 | tf_op jit(solution)/shard_map/mul | solution.py:503
Async XLA Ops:
  0.6 77.1 %copy-start = (f32[256]{0:T(256)S(1)}, f32[256]{0:T(256)}, u32[]{:S(2)}) copy-start(f32[256]{0:T(256)} %param.10) | copy-start | bytes 3076
